TPU v7x, 256 devices: a whole 4x4x8 slice. The times are simulated.
256 devices in a mesh: dp: 4 (over z_hi), row: 16 (over y, x), col: 4 (over z_lo, core).
Axes of the slice: x: 4, y: 4, z: 8 (z_hi: 4, z_lo: 2; z = z_hi * 2 + z_lo), core: 2. Of those that a mesh axis runs over, the one named last changes fastest.
Arguments:
- grad_partials: float32 [4, 4, 2048, 16384], P('dp', None, 'row', 'col'), may hold values from -300 to 300, as said below
- master_weights: float32 [8192, 16384], P(('dp', 'row'), 'col'), may hold values from -1.5 to 1.5
- row_moment: float32 [8192], P(('dp', 'row')), may hold values from 0.3 to 30
- col_moment: float32 [16384], P('col'), may hold values from 0.003 to 0.3
Outputs:
- new_master: float32 [8192, 16384], P(('dp', 'row'), 'col')
- new_row_moment: float32 [8192], P(('dp', 'row'))
- new_col_moment: float32 [16384], P('col')
- compute_weights: bfloat16 [4, 2048, 16384], P(None, 'row', 'col')
- rms_update: float32 [], replicated
Inputs may be any that keep to these rules, and one draw needn't show every extreme that they name: `grad_partials`: finite gradient partials.
All inputs are finite; a program needn't handle non-finite values.
Results may differ from a plain program's by a relative error of at most 0.0004.
Values may be sent and summed in bfloat16 or wider, within the bound.
A program may use at most 128 MiB of HBM per device.

v0:
```python
import jax
import jax.numpy as jnp
from jax import lax
from jax.sharding import PartitionSpec as P

decay_rate = 0.9
step_rate = 0.05
tiny_value = 1e-30


def local(grad_partials, master_weights, row_moment, col_moment):
    local_grads = grad_partials[0]
    row_dev = master_weights.shape[0]
    col_dev = master_weights.shape[1]
    groups = lax.axis_size("dp")
    all_rows = row_dev * groups * lax.axis_size("row")
    full_width = col_dev * lax.axis_size("col")
    summed = lax.psum_scatter(local_grads, "dp", scatter_dimension=0, tiled=True)
    gradient = summed.reshape(row_dev, col_dev)
    weights_all, moments_all = (master_weights, row_moment)
    squared = gradient * gradient
    row_totals = lax.psum(jnp.sum(squared, axis=1), "col")
    local_cols = jnp.sum(squared, axis=0)
    row_mean = row_totals / full_width + tiny_value
    new_rows = decay_rate * moments_all + (1.0 - decay_rate) * row_mean
    rows_sum = jnp.sum(new_rows)
    col_totals, moment_sum = lax.psum((local_cols, rows_sum), ("dp", "row"))
    col_mean = col_totals / all_rows + tiny_value
    new_cols = decay_rate * col_moment + (1.0 - decay_rate) * col_mean
    scale_mean = moment_sum / all_rows
    update = gradient * lax.rsqrt(new_rows[:, None] * new_cols[None, :] / scale_mean)
    update_local = jnp.sum(update * update)
    update_sum = lax.psum(update_local, ("dp", "row", "col"))
    entry_count = float(all_rows * full_width)
    rms_update = jnp.sqrt(update_sum / entry_count)
    new_weights = weights_all - step_rate * update / jnp.maximum(1.0, rms_update)
    copies = lax.all_gather(new_weights.astype(jnp.bfloat16)[None], "dp", axis=0, tiled=True)
    return (new_weights, new_rows, new_cols, copies, rms_update)


def solution(mesh):
    return jax.shard_map(
        local,
        mesh=mesh,
        in_specs=(P("dp", None, "row", "col"), P(("dp", "row"), "col"), P(("dp", "row")), P("col")),
        out_specs=(P(("dp", "row"), "col"), P(("dp", "row")), P("col"), P(None, "row", "col"), P()),
        check_vma=False,
    )
```

profile of v0, /device:TPU:37, one launch (start us, length us, event | category | flops | bytes accessed | tf_op | source)
XLA Modules:
  0.0 726.3 jit_solution(2824089146126804063)
XLA Ops:
  7.2 0.0 reduce-scatter.2.cloned.1.call-start
  7.2 0.7 reduce-scatter.2.cloned.1.call-update
  7.9 0.0 copy-start.4
  7.9 0.0 copy-start.2
  7.9 0.0 all-gather.3.cloned.1.call-start
  8.0 155.5 %reduce-scatter.2.cloned.1.call-done = f32[1,128,4096]{2,1,0:T(8,128)} async-done(((f32[4,128,4096]{2,1,0:T(8,128)}), f32[1,128,4096]{2,1,0:T(8,128)}) %reduce-scatter.2.cloned.1.call-update) | async-done | bytes 2097168 | tf_op jit(solution)/shard_map/reduce_scatter | solution.py:18
  163.5 0.0 copy-start
  163.5 2.0 fusion
  165.5 9.4 %psum.28 = f32[128]{0:T(128)S(1)} all-reduce(f32[128]{0:T(128)S(1)} %get-tuple-element.6), channel_id=1, replica_groups=mesh['dp'=4,'row'=16,'col'=4] {'col'}, use_global_device_ids=true, to_apply=%region_2.0 | all-reduce | flops 128 | bytes 1024 | tf_op jit(solution)/shard_map/psum | solution.py:22
  174.9 0.0 copy-done.4
  174.9 0.6 fusion.3
  175.5 0.0 copy-start.3
  175.5 313.2 %all-reduce = (f32[]{:T(128)}, f32[4096]{0:T(1024)S(1)}) all-reduce(f32[]{:T(128)} %get-tuple-element.11, f32[4096]{0:T(1024)S(1)} %get-tuple-element.5), channel_id=1, replica_groups=mesh['dp'=4,'row'=16,'col'=4] {'dp','row'}, use_global_device_ids=true, to_apply=%region_6.0 | all-reduce | flops 4097 | bytes 32776 | tf_op jit(solution)/shard_map/psum | solution.py:27
  489.4 0.0 copy-done.2
  489.4 0.0 copy-start.1
  489.4 0.0 copy-done
  489.4 1.2 multiply_reduce_fusion
  490.6 134.0 %psum.31 = f32[]{:T(128)} all-reduce(f32[]{:T(128)} %multiply_reduce_fusion), channel_id=1, replica_groups=mesh['dp'=4,'row'=16,'col'=4] {'dp','row','col'}, use_global_device_ids=true, to_apply=%region_8.0 | all-reduce | flops 1 | bytes 8 | tf_op jit(solution)/shard_map/psum | solution.py:33
  625.4 3.9 fusion.2
  629.3 0.0 copy-done.3
  629.3 0.0 copy-done.1
  629.3 0.0 all-gather.3.cloned.1.call-update
  629.3 84.4 %all-gather.3.cloned.1.call-done = bf16[512,4096]{1,0:T(8,128)(2,1)} async-done(((bf16[128,4096]{1,0:T(8,128)(2,1)}), bf16[512,4096]{1,0:T(8,128)(2,1)}) %all-gather.3.cloned.1.call-update) | async-done | bytes 4194320 | tf_op jit(solution)/shard_map/all_gather | solution.py:37
  713.6 4.7 copy.10
  (1 shorter events, 0.0 us)
Async XLA Ops:
  7.2 156.3 %reduce-scatter.2.cloned.1.call-start = ((), (), s32[]{:S(2)}) async-start(), calls=%async_computation.1 | async-start | bytes 10485760 | tf_op jit(solution)/shard_map/reduce_scatter | solution.py:18
  7.9 167.0 %copy-start.4 = (f32[128]{0:T(128)S(1)}, f32[128]{0:T(128)}, u32[]{:S(2)}) copy-start(f32[128]{0:T(128)} %param.6) | copy-start | bytes 1540
  7.9 481.4 %copy-start.2 = (f32[4096]{0:T(1024)S(1)}, f32[4096]{0:T(1024)}, u32[]{:S(2)}) copy-start(f32[4096]{0:T(1024)} %param.7) | copy-start | bytes 49156
  7.9 705.7 %all-gather.3.cloned.1.call-start = ((), (), s32[]{:S(2)}) async-start(), calls=%async_computation.2 | async-start | bytes 5242880 | tf_op jit(solution)/shard_map/all_gather | solution.py:37
  163.5 325.9 %copy-start = (f32[1,128,4096]{2,1,0:T(8,128)S(1)}, f32[1,128,4096]{2,1,0:T(8,128)}, u32[]{:S(2)}) copy-start(f32[1,128,4096]{2,1,0:T(8,128)} %reduce-scatter.2.cloned.1.call-done) | copy-start | bytes 6291460
  175.5 453.8 %copy-start.3 = (f32[128]{0:T(128)}, f32[128]{0:T(128)S(1)}, u32[]{:S(2)}) copy-start(f32[128]{0:T(128)S(1)} %get-tuple-element.19) | copy-start | bytes 1540
  489.4 139.9 %copy-start.1 = (f32[4096]{0:T(1024)}, f32[4096]{0:T(1024)S(1)}, u32[]{:S(2)}) copy-start(f32[4096]{0:T(1024)S(1)} %multiply_add_fusion) | copy-start | bytes 49156
Sparse Core Ops, SparseCore 0:
  10.6 152.8 reduce-scatter.1
  629.4 84.1 all-gather.2
where the time goes:
time: 727 us; the launch traced here: 726 us
  blocking collectives  457 us (63%)
  waiting for transfers between devices  241 us (33%)
  between operations  16.6 us (2%)
  other arithmetic  7.76 us (1%)
    psum x1, blocking collectives, local(): col_totals, moment_sum = lax.psum((local_cols, rows_sum), ('dp', 'row'))  313 us
    reduce_scatter x1, waiting for transfers between devices, local(): lax.psum_scatter(local_grads, 'dp', scatter_dimension=0, tiled=True)  155 us
    psum x1, blocking collectives, local(): update_sum = lax.psum(update_local, ('dp', 'row', 'col'))  134 us
    all_gather x1, waiting for transfers between devices, local(): lax.all_gather(new_weights.astype(jnp.bfloat16)[None], 'dp', axis=0, tile...  84.4 us
  transfers between devices with their start and end apart: 2, of which 2 were waited for; matrix products, arithmetic and copies ran while one was open for 0% of the time, Pallas kernels for 0%

commit v1 on v0

--- a/solution.py
+++ b/solution.py
@@ -24,7 +24,7 @@
     row_mean = row_totals / full_width + tiny_value
     new_rows = decay_rate * moments_all + (1.0 - decay_rate) * row_mean
     rows_sum = jnp.sum(new_rows)
-    col_totals, moment_sum = lax.psum((local_cols, rows_sum), ("dp", "row"))
+    col_totals, moment_sum = lax.psum(lax.psum((local_cols, rows_sum), "row"), "dp")
     col_mean = col_totals / all_rows + tiny_value
     new_cols = decay_rate * col_moment + (1.0 - decay_rate) * col_mean
     scale_mean = moment_sum / all_rows

time: 727 us -> 445 us (0.61)
  blocking collectives: 457 us -> 173 us
    psum x1 -> x2, blocking collectives: 313 us -> 70.7 us  [the longest x1 56.2 us: local(): lax.psum((local_cols, rows_sum), 'row')]
    psum x1, blocking collectives: 134 us -> 93.4 us  [local(): update_sum = lax.psum(update_local, ('dp', 'row', 'col'))]
where the time goes in v1:
time: 445 us; the launch traced here: 444 us
  waiting for transfers between devices  242 us (54%)
  blocking collectives  173 us (39%)
  between operations  16.6 us (4%)
  other arithmetic  7.76 us (2%)
  local copies, waits for them, and re-layouts  4.72 us (1%)
    reduce_scatter x1, waiting for transfers between devices, local(): lax.psum_scatter(local_grads, 'dp', scatter_dimension=0, tiled=True)  155 us
    psum x1, blocking collectives, local(): update_sum = lax.psum(update_local, ('dp', 'row', 'col'))  93.4 us
    all_gather x1, waiting for transfers between devices, local(): lax.all_gather(new_weights.astype(jnp.bfloat16)[None], 'dp', axis=0, tile...  85.6 us
    psum x1, blocking collectives, local(): lax.psum((local_cols, rows_sum), 'row')  56.2 us
    psum x1, blocking collectives, local(): lax.psum(lax.psum((local_cols, rows_sum), 'row'), 'dp')  14.5 us
    psum x1, blocking collectives, local(): row_totals = lax.psum(jnp.sum(squared, axis=1), 'col')  9.37 us
  transfers between devices with their start and end apart: 2, of which 2 were waited for; matrix products, arithmetic and copies ran while one was open for 0% of the time, Pallas kernels for 0%

profile of v1, /device:TPU:37, one launch (start us, length us, event | category | flops | bytes accessed | tf_op | source)
XLA Modules:
  0.0 444.4 jit_solution(15271801691491041260)
XLA Ops:
  7.2 0.0 reduce-scatter.2.cloned.1.call-start
  7.2 0.7 reduce-scatter.2.cloned.1.call-update
  7.9 0.0 copy-start.4
  7.9 0.0 copy-start.2
  7.9 0.0 all-gather.3.cloned.1.call-start
  8.0 155.5 %reduce-scatter.2.cloned.1.call-done = f32[1,128,4096]{2,1,0:T(8,128)} async-done(((f32[4,128,4096]{2,1,0:T(8,128)}), f32[1,128,4096]{2,1,0:T(8,128)}) %reduce-scatter.2.cloned.1.call-update) | async-done | bytes 2097168 | tf_op jit(solution)/shard_map/reduce_scatter | solution.py:18
  163.5 0.0 copy-start
  163.5 2.0 fusion
  165.5 9.4 %psum.42 = f32[128]{0:T(128)S(1)} all-reduce(f32[128]{0:T(128)S(1)} %get-tuple-element.6), channel_id=1, replica_groups=mesh['dp'=4,'row'=16,'col'=4] {'col'}, use_global_device_ids=true, to_apply=%region_2.0 | all-reduce | flops 128 | bytes 1024 | tf_op jit(solution)/shard_map/psum | solution.py:22
  174.9 0.0 copy-done.4
  174.9 0.6 fusion.3
  175.5 0.0 copy-start.3
  175.5 56.2 %all-reduce = (f32[]{:T(128)}, f32[4096]{0:T(1024)S(1)}) all-reduce(f32[]{:T(128)} %get-tuple-element.13, f32[4096]{0:T(1024)S(1)} %get-tuple-element.5), channel_id=1, replica_groups=mesh['dp'=4,'row'=16,'col'=4] {'row'}, use_global_device_ids=true, to_apply=%region_7.0 | all-reduce | flops 4097 | bytes 32776 | tf_op jit(solution)/shard_map/psum | solution.py:27
  231.7 14.5 %all-reduce.1 = (f32[]{:T(128)}, f32[4096]{0:T(1024)S(1)}) all-reduce(f32[]{:T(128)} %get-tuple-element.7, f32[4096]{0:T(1024)S(1)} %get-tuple-element.8), channel_id=1, replica_groups=mesh['dp'=4,'row'=16,'col'=4] {'dp'}, use_global_device_ids=true, to_apply=%region_8.0 | all-reduce | flops 4097 | bytes 32776 | tf_op jit(solution)/shard_map/psum | solution.py:27
  246.9 0.0 copy-done.2
  246.9 0.0 copy-start.1
  246.9 0.0 copy-done
  246.9 1.2 multiply_reduce_fusion
  248.2 93.4 %psum.47 = f32[]{:T(128)} all-reduce(f32[]{:T(128)} %multiply_reduce_fusion), channel_id=1, replica_groups=mesh['dp'=4,'row'=16,'col'=4] {'dp','row','col'}, use_global_device_ids=true, to_apply=%region_10.0 | all-reduce | flops 1 | bytes 8 | tf_op jit(solution)/shard_map/psum | solution.py:33
  342.2 3.9 fusion.2
  346.1 0.0 copy-done.3
  346.1 0.0 copy-done.1
  346.1 0.0 all-gather.3.cloned.1.call-update
  346.1 85.6 %all-gather.3.cloned.1.call-done = bf16[512,4096]{1,0:T(8,128)(2,1)} async-done(((bf16[128,4096]{1,0:T(8,128)(2,1)}), bf16[512,4096]{1,0:T(8,128)(2,1)}) %all-gather.3.cloned.1.call-update) | async-done | bytes 4194320 | tf_op jit(solution)/shard_map/all_gather | solution.py:37
  431.7 4.7 %copy.10 = bf16[4,128,4096]{2,1,0:T(8,128)(2,1)} copy(bf16[4,128,4096]{2,1,0:T(8,128)(2,1)} %bitcast.15) | data formatting | bytes 8388608
  (1 shorter events, 0.0 us)
Async XLA Ops:
  7.2 156.3 %reduce-scatter.2.cloned.1.call-start = ((), (), s32[]{:S(2)}) async-start(), calls=%async_computation.1 | async-start | bytes 10485760 | tf_op jit(solution)/shard_map/reduce_scatter | solution.py:18
  7.9 167.0 %copy-start.4 = (f32[128]{0:T(128)S(1)}, f32[128]{0:T(128)}, u32[]{:S(2)}) copy-start(f32[128]{0:T(128)} %param.6) | copy-start | bytes 1540
  7.9 239.0 %copy-start.2 = (f32[4096]{0:T(1024)S(1)}, f32[4096]{0:T(1024)}, u32[]{:S(2)}) copy-start(f32[4096]{0:T(1024)} %param.7) | copy-start | bytes 49156
  7.9 423.8 %all-gather.3.cloned.1.call-start = ((), (), s32[]{:S(2)}) async-start(), calls=%async_computation.2 | async-start | bytes 5242880 | tf_op jit(solution)/shard_map/all_gather | solution.py:37
  163.5 83.5 %copy-start = (f32[1,128,4096]{2,1,0:T(8,128)S(1)}, f32[1,128,4096]{2,1,0:T(8,128)}, u32[]{:S(2)}) copy-start(f32[1,128,4096]{2,1,0:T(8,128)} %reduce-scatter.2.cloned.1.call-done) | copy-start | bytes 6291460
  175.5 170.6 %copy-start.3 = (f32[128]{0:T(128)}, f32[128]{0:T(128)S(1)}, u32[]{:S(2)}) copy-start(f32[128]{0:T(128)S(1)} %get-tuple-element.21) | copy-start | bytes 1540
  246.9 99.2 %copy-start.1 = (f32[4096]{0:T(1024)}, f32[4096]{0:T(1024)S(1)}, u32[]{:S(2)}) copy-start(f32[4096]{0:T(1024)S(1)} %multiply_add_fusion) | copy-start | bytes 49156
Sparse Core Ops, SparseCore 0:
  10.6 152.8 reduce-scatter.1
  346.2 85.4 all-gather.2
